TPU v7x, 32 devices: a whole 2x2x4 slice. The times are simulated.
32 devices in a mesh: wide: 8 (over y, x, core), by: 4 (over z).
Axes of the slice: x: 2, y: 2, z: 4, core: 2. Of those that a mesh axis runs over, the one named last changes fastest.
Arguments:
- tiles: float32 [704, 512, 512], P(('wide', 'by')), may hold values from -6 to 6
- tile_rows: int32 [704], P(('wide', 'by')), may hold values from 0 to 7
- tile_cols: int32 [704], P(('wide', 'by')), may hold values from 0 to 63, as said below
- start_panel: float32 [32768, 64], P('wide'), may hold values from -6 to 6
Outputs:
- panel: float32 [32768, 64], P('wide')
- factor: float32 [64, 64], replicated
Inputs may be any that keep to these rules, and one draw needn't show every extreme that they name: `tile_cols`: within one device's 22 tiles, at most 3 have block columns in the block rows of one index of wide, and one index of wide takes exactly 3 of them.
All inputs are finite; a program needn't handle non-finite values.
Results may differ from a plain program's by a relative error of at most 0.0001.
Values sent between devices are 32-bit elements; how exact they have to be, the bound alone decides.
No kernel may reach another device: no remote copies, remote signals or barrier semaphores. Data moves between devices by JAX's collectives and lax.ppermute only.
A program may use at most 192 MiB of HBM per device.

v0:
```python
import jax
import jax.numpy as jnp
from jax import lax
from jax.sharding import PartitionSpec as P

ITERS = 2


def local(tiles, tile_rows, tile_cols, start_panel):
    wide_count = lax.axis_size("wide")
    my_wide = lax.axis_index("wide")
    tile_count = tiles.shape[0]
    block_size = tiles.shape[1]
    width = start_panel.shape[1]
    block_rows = start_panel.shape[0] // block_size
    capacity = max(2, tile_count // wide_count + 1)
    slot_count = wide_count * capacity
    highest = lax.Precision.HIGHEST
    peer_index = tile_cols // block_rows
    positions = jnp.arange(tile_count, dtype=jnp.int32)
    earlier = positions[:, None] > positions[None, :]
    same_peer = peer_index[:, None] == peer_index[None, :]
    rank_within = jnp.sum((earlier & same_peer).astype(jnp.int32), axis=1)
    slot_of = peer_index * capacity + rank_within
    slot_match = slot_of[:, None] == jnp.arange(slot_count, dtype=jnp.int32)[None, :]
    slot_table = slot_match.astype(jnp.float32)
    request = jnp.sum(jnp.where(slot_match, tile_cols[:, None] + 1, 0), axis=0) - 1
    incoming = lax.all_to_all(
        request.reshape(wide_count, capacity), "wide", split_axis=0, concat_axis=0, tiled=True
    ).reshape(slot_count)
    local_in = incoming - my_wide * block_rows
    block_iota = jnp.arange(block_rows, dtype=jnp.int32)
    serve_table = (local_in[:, None] == block_iota[None, :]).astype(jnp.float32)
    row_table = (tile_rows[:, None] == block_iota[None, :]).astype(jnp.float32)
    panel = start_panel
    factor = jnp.zeros((width, width), jnp.float32)
    for step in range(ITERS):
        flat_panel = panel.reshape(block_rows, block_size * width)
        outgoing = jnp.dot(serve_table, flat_panel, precision=highest)
        received = lax.all_to_all(outgoing, "wide", split_axis=0, concat_axis=0, tiled=True)
        col_panels = jnp.dot(slot_table, received, precision=highest).reshape(
            tile_count, block_size, width
        )
        row_panels = jnp.dot(row_table, flat_panel, precision=highest).reshape(
            tile_count, block_size, width
        )
        direct = jnp.einsum("tab,tbk->tak", tiles, col_panels, precision=highest)
        mirror = jnp.einsum("tba,tbk->tak", tiles, row_panels, precision=highest)
        partial_rows = jnp.dot(
            row_table.T, direct.reshape(tile_count, block_size * width), precision=highest
        )
        mirror_flat = mirror.reshape(tile_count, block_size * width)
        placed = jnp.dot(slot_table.T, mirror_flat, precision=highest)
        returned = lax.all_to_all(placed, "wide", split_axis=0, concat_axis=0, tiled=True)
        partial_rows = partial_rows + jnp.dot(serve_table.T, returned, precision=highest)
        partial_rows = partial_rows.reshape(block_rows * block_size, width)
        image = lax.psum(partial_rows, "by")
        gram = lax.psum(jnp.dot(image.T, image, precision=highest), "wide")
        factor = jnp.linalg.cholesky(gram)
        panel = jax.scipy.linalg.solve_triangular(factor, image.T, lower=True).T
    return (panel, factor)


def solution(mesh):
    placed = (P(("wide", "by"), None, None), P(("wide", "by")), P(("wide", "by")), P("wide", None))
    return jax.shard_map(
        local, mesh=mesh, in_specs=placed, out_specs=(P("wide", None), P()), check_vma=False
    )
```

profile of v0, /device:TPU:0, one launch (start us, length us, event | category | flops | bytes accessed | tf_op | source)
XLA Modules:
  0.0 638.6 jit_solution(3037137050593948503)
XLA Ops:
  8.8 5.2 all-to-all-start
  22.6 21.3 %fusion.13 = f32[22,512,64]{1,2,0:T(8,128)} fusion(f32[22,512,512]{2,1,0:T(8,128)} %param.7, f32[22,512,64]{1,0,2:T(8,128)S(1)} %fusion.60), kind=kOutput, calls=%fused_computation.15 | convolution fusion | flops 4429185024 | bytes 28835840 | tf_op jit(solution)/shard_map/tba,tbk->tak/dot_general | solution.py:48
  43.9 5.3 copy.59
  49.2 6.3 reshape.153
  63.2 4.5 all-to-all-start.2
  75.3 41.6 %all-to-all-done.2 = f32[8,3,32768]{2,1,0:T(4,128)} async-done(((f32[8,3,32768]{2,1,0:T(4,128)}), f32[8,3,32768]{2,1,0:T(4,128)}, u32[]{:S(2)}, u32[]{:S(2)}) %all-to-all-start.2) | async-done | bytes 3145760 | tf_op jit(solution)/shard_map/all_to_all | solution.py:54
  116.9 4.5 all-to-all-start.1
  125.3 45.2 %all-to-all-done.1 = f32[8,3,32768]{2,1,0:T(4,128)} async-done(((f32[8,3,32768]{2,1,0:T(4,128)}), f32[8,3,32768]{2,1,0:T(4,128)}, u32[]{:S(2)}, u32[]{:S(2)}) %all-to-all-start.1) | async-done | bytes 3145760 | tf_op jit(solution)/shard_map/all_to_all | solution.py:40
  170.5 5.5 all_to_all.30
  176.0 6.4 %dot_general.80 = f32[512,64,24]{1,0,2:T(8,128)} reshape(f32[32768,24]{0,1:T(8,128)} %bitcast.82) | data formatting | bytes 6291456 | tf_op jit(solution)/shard_map/dot_general | solution.py:41
  182.4 6.6 %copy.54 = f32[512,64,24]{0,2,1:T(8,128)} copy(f32[512,64,24]{1,0,2:T(8,128)} %dot_general.80) | data formatting | bytes 6291456 | tf_op jit(solution)/shard_map/dot_general | solution.py:41
  192.6 27.3 %fusion.10 = f32[22,512,64]{1,2,0:T(8,128)} fusion(f32[22,512,512]{2,1,0:T(8,128)} %param.7, f32[22,512,64]{1,0,2:T(8,128)S(1)} %fusion.37), kind=kOutput, calls=%fused_computation.14 | convolution fusion | flops 4429185024 | bytes 28835840 | tf_op jit(solution)/shard_map/tab,tbk->tak/dot_general | solution.py:47
  219.9 5.3 copy.56
  225.3 6.5 %reshape.143 = f32[22,32768]{1,0:T(8,128)} reshape(f32[22,512,64]{2,1,0:T(8,128)} %copy.56) | data formatting | bytes 5767168 | tf_op jit(solution)/shard_map/reshape | solution.py:50
  240.5 86.1 %all-reduce.3.cloned.1.call-done = f32[4096,64]{1,0:T(8,128)} async-done(((f32[4096,64]{1,0:T(8,128)}), f32[4096,64]{1,0:T(8,128)}) %all-reduce.3.cloned.1.call-update) | async-done | bytes 1048592 | tf_op jit(solution)/shard_map/psum | solution.py:57
  326.6 5.9 fusion.68
  332.5 24.3 %psum.29 = f32[64,64]{0,1:T(8,128)S(1)} all-reduce(f32[64,64]{0,1:T(8,128)S(1)} %fusion.68), channel_id=1, replica_groups=mesh['wide'=8,'by'=4] {'wide'}, use_global_device_ids=true, to_apply=%region_3.4 | all-reduce | flops 4096 | bytes 32768 | tf_op jit(solution)/shard_map/psum | solution.py:58
  356.9 5.8 cholesky.44
  364.1 4.9 custom-call.6
  378.2 4.8 all-to-all-start.3
  386.9 19.4 %fusion.19 = f32[22,512,64]{1,2,0:T(8,128)S(1)} fusion(f32[22,512,512]{2,1,0:T(8,128)} %param.7, f32[22,512,64]{1,0,2:T(8,128)S(1)} %fusion.58), kind=kOutput, calls=%fused_computation.17 | convolution fusion | flops 4429185024 | bytes 28835840 | tf_op jit(solution)/shard_map/tba,tbk->tak/dot_general | solution.py:48
  410.2 4.6 reshape.155
  420.5 11.6 %all-to-all-done.3 = f32[8,3,32768]{2,1,0:T(4,128)} async-done(((f32[8,3,32768]{2,1,0:T(4,128)}), f32[8,3,32768]{2,1,0:T(4,128)}, u32[]{:S(2)}, u32[]{:S(2)}) %all-to-all-start.3) | async-done | bytes 3145760 | tf_op jit(solution)/shard_map/all_to_all | solution.py:40
  432.2 4.5 all-to-all-start.4
  440.5 4.9 dot_general.95
  445.4 5.0 copy.65
  452.1 25.6 %fusion.16 = f32[22,512,64]{1,2,0:T(8,128)S(1)} fusion(f32[22,512,512]{2,1,0:T(8,128)} %param.7, f32[22,512,64]{1,0,2:T(8,128)S(1)} %fusion.35), kind=kOutput, calls=%fused_computation.16 | convolution fusion | flops 4429185024 | bytes 28835840 | tf_op jit(solution)/shard_map/tab,tbk->tak/dot_general | solution.py:47
  498.9 86.2 %all-reduce.5.cloned.1.call-done = f32[4096,64]{1,0:T(8,128)} async-done(((f32[4096,64]{1,0:T(8,128)}), f32[4096,64]{1,0:T(8,128)}) %all-reduce.5.cloned.1.call-update) | async-done | bytes 1048592 | tf_op jit(solution)/shard_map/psum | solution.py:57
  585.1 5.9 fusion.69
  591.0 24.4 %psum.31 = f32[64,64]{0,1:T(8,128)S(1)} all-reduce(f32[64,64]{0,1:T(8,128)S(1)} %fusion.69), channel_id=1, replica_groups=mesh['wide'=8,'by'=4] {'wide'}, use_global_device_ids=true, to_apply=%region_7.10 | all-reduce | flops 4096 | bytes 32768 | tf_op jit(solution)/shard_map/psum | solution.py:58
  615.5 5.8 cholesky.55
  623.3 4.9 custom-call.7
  (69 shorter events, 97.6 us)
Async XLA Ops:
  8.8 54.4 %all-to-all-start = ((s32[8,1,3]{2,1,0:T(1,128)}), s32[8,1,3]{2,1,0:T(1,128)S(1)}, u32[]{:S(2)}, u32[]{:S(2)}) async-start(s32[8,1,3]{2,1,0:T(1,128)} %bitcast.1), calls=%async_computation | async-start | bytes 8192 | tf_op jit(solution)/shard_map/all_to_all | solution.py:28
  16.5 4.7 copy-start.2
  63.2 53.7 %all-to-all-start.2 = ((f32[8,3,32768]{2,1,0:T(4,128)}), f32[8,3,32768]{2,1,0:T(4,128)}, u32[]{:S(2)}, u32[]{:S(2)}) async-start(f32[8,3,32768]{2,1,0:T(4,128)} %copy.60), calls=%async_computation.2 | async-start | bytes 8388608 | tf_op jit(solution)/shard_map/all_to_all | solution.py:54
  116.9 53.7 %all-to-all-start.1 = ((f32[8,3,32768]{2,1,0:T(4,128)}), f32[8,3,32768]{2,1,0:T(4,128)}, u32[]{:S(2)}, u32[]{:S(2)}) async-start(f32[8,3,32768]{2,1,0:T(4,128)} %copy.53), calls=%async_computation.1 | async-start | bytes 8388608 | tf_op jit(solution)/shard_map/all_to_all | solution.py:40
  121.4 205.1 %all-reduce.3.cloned.1.call-start = ((), (), s32[]{:S(2)}) async-start(), calls=%async_computation.5 | async-start | bytes 4194304 | tf_op jit(solution)/shard_map/psum | solution.py:57
  326.6 42.5 %copy-start.1 = (f32[4096,64]{1,0:T(8,128)S(1)}, f32[4096,64]{1,0:T(8,128)}, u32[]{:S(2)}) copy-start(f32[4096,64]{1,0:T(8,128)} %all-reduce.3.cloned.1.call-done) | copy-start | bytes 3145732
  378.2 54.0 %all-to-all-start.3 = ((f32[8,3,32768]{2,1,0:T(4,128)}), f32[8,3,32768]{2,1,0:T(4,128)}, u32[]{:S(2)}, u32[]{:S(2)}) async-start(f32[8,3,32768]{2,1,0:T(4,128)} %copy.64), calls=%async_computation.3 | async-start | bytes 8388608 | tf_op jit(solution)/shard_map/all_to_all | solution.py:40
  432.2 56.1 %all-to-all-start.4 = ((f32[8,3,32768]{2,1,0:T(4,128)}), f32[8,3,32768]{2,1,0:T(4,128)}, u32[]{:S(2)}, u32[]{:S(2)}) async-start(f32[8,3,32768]{2,1,0:T(4,128)} %copy.71), calls=%async_computation.4 | async-start | bytes 8388608 | tf_op jit(solution)/shard_map/all_to_all | solution.py:54
  436.7 148.4 %all-reduce.5.cloned.1.call-start = ((), (), s32[]{:S(2)}) async-start(), calls=%async_computation.6 | async-start | bytes 4194304 | tf_op jit(solution)/shard_map/psum | solution.py:57
  585.1 43.1 %copy-start = (f32[4096,64]{1,0:T(8,128)S(1)}, f32[4096,64]{1,0:T(8,128)}, u32[]{:S(2)}) copy-start(f32[4096,64]{1,0:T(8,128)} %all-reduce.5.cloned.1.call-done) | copy-start | bytes 3145732
Sparse Core Ops, SparseCore 0:
  240.6 85.9 all-reduce.2
  499.0 86.0 all-reduce.4
where the time goes:
time: 648 us; the launch traced here: 639 us
  waiting for transfers between devices  271 us (42%)
  matrix products  138 us (21%)
  local copies, waits for them, and re-layouts  116 us (18%)
  blocking collectives  48.7 us (8%)
  other arithmetic  26.4 us (4%)
  starting transfers between devices  23.7 us (4%)
  between operations  14.6 us (2%)
    psum x2, waiting for transfers between devices, local(): image = lax.psum(partial_rows, 'by')  172 us
    all_to_all x2, waiting for transfers between devices, local(): lax.all_to_all(outgoing, 'wide', split_axis=0, concat_axis=0, tiled=True)  56.9 us
    dot_general x2, matrix products, local(): direct = jnp.einsum('tab,tbk->tak', tiles, col_panels, precision=highest)  52.9 us
    psum x2, blocking collectives, local(): gram = lax.psum(jnp.dot(image.T, image, precision=highest), 'wide')  48.7 us
    all_to_all x2, waiting for transfers between devices, local(): lax.all_to_all(placed, 'wide', split_axis=0, concat_axis=0, tiled=True)  41.6 us
    dot_general x2, matrix products, local(): mirror = jnp.einsum('tba,tbk->tak', tiles, row_panels, precision=highest)  40.7 us
    dot_general x4, local copies, waits for them, and re-layouts, local(): jnp.dot(slot_table, received, precision=highest)  22.9 us
    another operation x6, other arithmetic, local(): factor = jnp.linalg.cholesky(gram)  13 us
  transfers between devices with their start and end apart: 7, of which 5 were waited for; matrix products, arithmetic and copies ran while one was open for 22% of the time, Pallas kernels for 0%

commit v1 on v0

--- a/solution.py
+++ b/solution.py
@@ -54,7 +54,9 @@
         returned = lax.all_to_all(placed, "wide", split_axis=0, concat_axis=0, tiled=True)
         partial_rows = partial_rows + jnp.dot(serve_table.T, returned, precision=highest)
         partial_rows = partial_rows.reshape(block_rows * block_size, width)
-        image = lax.psum(partial_rows, "by")
+        image = partial_rows
+        for hop in (1, 2):
+            image = image + lax.ppermute(image, "by", [(dev, dev ^ hop) for dev in range(4)])
         gram = lax.psum(jnp.dot(image.T, image, precision=highest), "wide")
         factor = jnp.linalg.cholesky(gram)
         panel = jax.scipy.linalg.solve_triangular(factor, image.T, lower=True).T

time: 648 us -> 627 us (0.968)
  waiting for transfers between devices: 271 us -> 231 us
  between operations: 14.6 us -> 1.18 us
  local copies, waits for them, and re-layouts: 116 us -> 127 us
  starting transfers between devices: 23.7 us -> 33.6 us
    psum x2 -> x0, waiting for transfers between devices: 172 us -> none  [local(): image = lax.psum(partial_rows, 'by')]
    ppermute x0 -> x4, waiting for transfers between devices: none -> 132 us  [local(): lax.ppermute(image, 'by', [(dev, dev ^ hop) for dev in range(4)])]
    ppermute x0 -> x4, starting transfers between devices: none -> 9.31 us  [local(): lax.ppermute(image, 'by', [(dev, dev ^ hop) for dev in range(4)])]
    ppermute x0 -> x4, local copies, waits for them, and re-layouts: none -> 7.73 us  [local(): lax.ppermute(image, 'by', [(dev, dev ^ hop) for dev in range(4)])]
  transfers between devices with their start and end apart: 7 -> 9, of which waited for: 5 -> 7; matrix products, arithmetic and copies ran while one was open for 22% -> 23% of each run, Pallas kernels for 0% -> 0%
where the time goes in v1:
time: 627 us; the launch traced here: 617 us
  waiting for transfers between devices  231 us (37%)
  matrix products  142 us (23%)
  local copies, waits for them, and re-layouts  127 us (20%)
  blocking collectives  51.3 us (8%)
  starting transfers between devices  33.6 us (5%)
  other arithmetic  31.3 us (5%)
    ppermute x4, waiting for transfers between devices, local(): lax.ppermute(image, 'by', [(dev, dev ^ hop) for dev in range(4)])  132 us
    all_to_all x2, waiting for transfers between devices, local(): lax.all_to_all(outgoing, 'wide', split_axis=0, concat_axis=0, tiled=True)  57.2 us
    dot_general x2, matrix products, local(): direct = jnp.einsum('tab,tbk->tak', tiles, col_panels, precision=highest)  53 us
    psum x2, blocking collectives, local(): gram = lax.psum(jnp.dot(image.T, image, precision=highest), 'wide')  51.3 us
    all_to_all x2, waiting for transfers between devices, local(): lax.all_to_all(placed, 'wide', split_axis=0, concat_axis=0, tiled=True)  41.6 us
    dot_general x2, matrix products, local(): mirror = jnp.einsum('tba,tbk->tak', tiles, row_panels, precision=highest)  40.7 us
    dot_general x4, local copies, waits for them, and re-layouts, local(): jnp.dot(slot_table, received, precision=highest)  22.3 us
    another operation x6, other arithmetic, local(): factor = jnp.linalg.cholesky(gram)  13 us
  transfers between devices with their start and end apart: 9, of which 7 were waited for; matrix products, arithmetic and copies ran while one was open for 23% of the time, Pallas kernels for 0%

profile of v1, /device:TPU:0, one launch (start us, length us, event | category | flops | bytes accessed | tf_op | source)
XLA Modules:
  0.0 617.1 jit_solution(1070326861681144036)
XLA Ops:
  2.3 5.2 all-to-all-start
  16.1 21.3 %fusion.13 = f32[22,512,64]{1,2,0:T(8,128)} fusion(f32[22,512,512]{2,1,0:T(8,128)} %param.7, f32[22,512,64]{1,0,2:T(8,128)S(1)} %fusion.66), kind=kOutput, calls=%fused_computation.15 | convolution fusion | flops 4429185024 | bytes 28835840 | tf_op jit(solution)/shard_map/tba,tbk->tak/dot_general | solution.py:48
  37.4 5.3 copy.67
  42.7 6.4 %reshape.153 = f32[22,32768,1]{1,0,2:T(8,128)} reshape(f32[22,512,64]{2,1,0:T(8,128)} %copy.67) | data formatting | bytes 5767168 | tf_op jit(solution)/shard_map/reshape | solution.py:52
  68.8 41.6 %all-to-all-done.2 = f32[8,3,32768]{2,1,0:T(4,128)} async-done(((f32[8,3,32768]{2,1,0:T(4,128)}), f32[8,3,32768]{2,1,0:T(4,128)}, u32[]{:S(2)}, u32[]{:S(2)}) %all-to-all-start.2) | async-done | bytes 3145760 | tf_op jit(solution)/shard_map/all_to_all | solution.py:54
  110.5 5.1 all-to-all-start.1
  119.4 45.3 %all-to-all-done.1 = f32[8,3,32768]{2,1,0:T(4,128)} async-done(((f32[8,3,32768]{2,1,0:T(4,128)}), f32[8,3,32768]{2,1,0:T(4,128)}, u32[]{:S(2)}, u32[]{:S(2)}) %all-to-all-start.1) | async-done | bytes 3145760 | tf_op jit(solution)/shard_map/all_to_all | solution.py:40
  164.7 5.5 all_to_all.30
  170.1 6.2 %dot_general.80 = f32[512,64,24]{1,0,2:T(8,128)} reshape(f32[32768,24]{0,1:T(8,128)} %bitcast.78) | data formatting | bytes 6291456 | tf_op jit(solution)/shard_map/dot_general | solution.py:41
  176.3 6.6 %copy.62 = f32[512,64,24]{0,2,1:T(8,128)} copy(f32[512,64,24]{1,0,2:T(8,128)} %dot_general.80) | data formatting | bytes 6291456 | tf_op jit(solution)/shard_map/dot_general | solution.py:41
  186.5 27.5 %fusion.10 = f32[22,512,64]{1,2,0:T(8,128)} fusion(f32[22,512,512]{2,1,0:T(8,128)} %param.7, f32[22,512,64]{1,0,2:T(8,128)S(1)} %fusion.43), kind=kOutput, calls=%fused_computation.14 | convolution fusion | flops 4429185024 | bytes 28835840 | tf_op jit(solution)/shard_map/tab,tbk->tak/dot_general | solution.py:47
  214.0 5.3 copy.64
  219.4 6.3 %reshape.143 = f32[22,32768]{1,0:T(8,128)} reshape(f32[22,512,64]{2,1,0:T(8,128)} %copy.64) | data formatting | bytes 5767168 | tf_op jit(solution)/shard_map/reshape | solution.py:50
  236.3 20.6 %collective-permute-done = f32[4096,64]{0,1:T(8,128)S(1)} collective-permute-done((f32[4096,64]{0,1:T(8,128)}, f32[4096,64]{0,1:T(8,128)S(1)}, u32[]{:S(2)}, u32[]{:S(2)}) %collective-permute-start) | collective-permute-done | bytes 1048608 | tf_op jit(solution)/shard_map/ppermute | solution.py:59
  265.4 42.0 %collective-permute-done.1 = f32[4096,64]{0,1:T(8,128)S(1)} collective-permute-done((f32[4096,64]{0,1:T(8,128)}, f32[4096,64]{0,1:T(8,128)S(1)}, u32[]{:S(2)}, u32[]{:S(2)}) %collective-permute-start.1) | collective-permute-done | bytes 1048608 | tf_op jit(solution)/shard_map/ppermute | solution.py:59
  309.4 5.9 fusion.26
  315.2 27.6 %psum.14 = f32[64,64]{0,1:T(8,128)S(1)} all-reduce(f32[64,64]{0,1:T(8,128)S(1)} %fusion.26), channel_id=1, replica_groups=mesh['wide'=8,'by'=4] {'wide'}, use_global_device_ids=true, to_apply=%region_2.3 | all-reduce | flops 4096 | bytes 32768 | tf_op jit(solution)/shard_map/psum | solution.py:60
  343.0 5.8 cholesky.44
  350.2 4.9 custom-call.6
  365.9 4.8 all-to-all-start.3
  374.5 19.4 %fusion.19 = f32[22,512,64]{1,2,0:T(8,128)S(1)} fusion(f32[22,512,512]{2,1,0:T(8,128)} %param.7, f32[22,512,64]{1,0,2:T(8,128)S(1)} %fusion.64), kind=kOutput, calls=%fused_computation.17 | convolution fusion | flops 4429185024 | bytes 28835840 | tf_op jit(solution)/shard_map/tba,tbk->tak/dot_general | solution.py:48
  407.9 11.9 %all-to-all-done.3 = f32[8,3,32768]{2,1,0:T(4,128)} async-done(((f32[8,3,32768]{2,1,0:T(4,128)}), f32[8,3,32768]{2,1,0:T(4,128)}, u32[]{:S(2)}, u32[]{:S(2)}) %all-to-all-start.3) | async-done | bytes 3145760 | tf_op jit(solution)/shard_map/all_to_all | solution.py:40
  419.8 4.8 all-to-all-start.4
  432.8 5.0 copy.77
  439.5 25.6 %fusion.16 = f32[22,512,64]{1,2,0:T(8,128)S(1)} fusion(f32[22,512,512]{2,1,0:T(8,128)} %param.7, f32[22,512,64]{1,0,2:T(8,128)S(1)} %fusion.41), kind=kOutput, calls=%fused_computation.16 | convolution fusion | flops 4429185024 | bytes 28835840 | tf_op jit(solution)/shard_map/tab,tbk->tak/dot_general | solution.py:47
  488.7 24.0 %collective-permute-done.2 = f32[4096,64]{0,1:T(8,128)S(1)} collective-permute-done((f32[4096,64]{0,1:T(8,128)}, f32[4096,64]{0,1:T(8,128)S(1)}, u32[]{:S(2)}, u32[]{:S(2)}) %collective-permute-start.2) | collective-permute-done | bytes 1048608 | tf_op jit(solution)/shard_map/ppermute | solution.py:59
  521.8 45.9 %collective-permute-done.3 = f32[4096,64]{0,1:T(8,128)S(1)} collective-permute-done((f32[4096,64]{0,1:T(8,128)}, f32[4096,64]{0,1:T(8,128)S(1)}, u32[]{:S(2)}, u32[]{:S(2)}) %collective-permute-start.3) | collective-permute-done | bytes 1048608 | tf_op jit(solution)/shard_map/ppermute | solution.py:59
  569.6 5.9 fusion.23
  575.5 23.6 %psum.15 = f32[64,64]{0,1:T(8,128)S(1)} all-reduce(f32[64,64]{0,1:T(8,128)S(1)} %fusion.23), channel_id=1, replica_groups=mesh['wide'=8,'by'=4] {'wide'}, use_global_device_ids=true, to_apply=%region_5.8 | all-reduce | flops 4096 | bytes 32768 | tf_op jit(solution)/shard_map/psum | solution.py:60
  599.2 5.8 cholesky.55
  607.0 4.9 custom-call.7
  611.9 4.9 convolution_bitcast_fusion
  (81 shorter events, 135.2 us)
Async XLA Ops:
  2.3 54.5 %all-to-all-start = ((s32[8,1,3]{2,1,0:T(1,128)}), s32[8,1,3]{2,1,0:T(1,128)S(1)}, u32[]{:S(2)}, u32[]{:S(2)}) async-start(s32[8,1,3]{2,1,0:T(1,128)} %bitcast.1), calls=%async_computation | async-start | bytes 8192 | tf_op jit(solution)/shard_map/all_to_all | solution.py:28
  9.9 4.7 copy-start.2
  56.8 53.7 %all-to-all-start.2 = ((f32[8,3,32768]{2,1,0:T(4,128)}), f32[8,3,32768]{2,1,0:T(4,128)}, u32[]{:S(2)}, u32[]{:S(2)}) async-start(f32[8,3,32768]{2,1,0:T(4,128)} %copy.68), calls=%async_computation.2 | async-start | bytes 8388608 | tf_op jit(solution)/shard_map/all_to_all | solution.py:54
  110.5 54.2 %all-to-all-start.1 = ((f32[8,3,32768]{2,1,0:T(4,128)}), f32[8,3,32768]{2,1,0:T(4,128)}, u32[]{:S(2)}, u32[]{:S(2)}) async-start(f32[8,3,32768]{2,1,0:T(4,128)} %copy.61), calls=%async_computation.1 | async-start | bytes 8388608 | tf_op jit(solution)/shard_map/all_to_all | solution.py:40
  233.1 23.8 %copy-start = (f32[4096,64]{1,0:T(8,128)}, f32[4096,64]{1,0:T(8,128)S(1)}, u32[]{:S(2)}) copy-start(f32[4096,64]{1,0:T(8,128)S(1)} %reshape.145) | copy-start | bytes 3145732
  234.8 22.1 %collective-permute-start = (f32[4096,64]{0,1:T(8,128)}, f32[4096,64]{0,1:T(8,128)S(1)}, u32[]{:S(2)}, u32[]{:S(2)}) collective-permute-start(f32[4096,64]{0,1:T(8,128)} %copy.69), channel_id=1, source_target_pairs={{0,1},{1,0},{2,3},{3,2},{4,5},{5,4},{6,7},{7,6},{8,9},{9,8},{10,11... | collective-permute-start | bytes 3145736 | tf_op jit(solution)/shard_map/ppermute | solution.py:59
  262.8 44.6 %collective-permute-start.1 = (f32[4096,64]{0,1:T(8,128)}, f32[4096,64]{0,1:T(8,128)S(1)}, u32[]{:S(2)}, u32[]{:S(2)}) collective-permute-start(f32[4096,64]{0,1:T(8,128)} %copy.71), channel_id=1, source_target_pairs={{0,2},{1,3},{2,0},{3,1},{4,6},{5,7},{6,4},{7,5},{8,10},{9,11},{10,... | collective-permute-start | bytes 3145736 | tf_op jit(solution)/shard_map/ppermute | solution.py:59
  365.9 53.9 %all-to-all-start.3 = ((f32[8,3,32768]{2,1,0:T(4,128)}), f32[8,3,32768]{2,1,0:T(4,128)}, u32[]{:S(2)}, u32[]{:S(2)}) async-start(f32[8,3,32768]{2,1,0:T(4,128)} %copy.76), calls=%async_computation.3 | async-start | bytes 8388608 | tf_op jit(solution)/shard_map/all_to_all | solution.py:40
  419.8 56.1 %all-to-all-start.4 = ((f32[8,3,32768]{2,1,0:T(4,128)}), f32[8,3,32768]{2,1,0:T(4,128)}, u32[]{:S(2)}, u32[]{:S(2)}) async-start(f32[8,3,32768]{2,1,0:T(4,128)} %copy.83), calls=%async_computation.4 | async-start | bytes 8388608 | tf_op jit(solution)/shard_map/all_to_all | solution.py:54
  485.1 27.5 %copy-start.1 = (f32[4096,64]{1,0:T(8,128)}, f32[4096,64]{1,0:T(8,128)S(1)}, u32[]{:S(2)}) copy-start(f32[4096,64]{1,0:T(8,128)S(1)} %reshape.149) | copy-start | bytes 3145732
  486.8 25.8 %collective-permute-start.2 = (f32[4096,64]{0,1:T(8,128)}, f32[4096,64]{0,1:T(8,128)S(1)}, u32[]{:S(2)}, u32[]{:S(2)}) collective-permute-start(f32[4096,64]{0,1:T(8,128)} %copy.84), channel_id=1, source_target_pairs={{0,1},{1,0},{2,3},{3,2},{4,5},{5,4},{6,7},{7,6},{8,9},{9,8},{10,11... | collective-permute-start | bytes 3145736 | tf_op jit(solution)/shard_map/ppermute | solution.py:59
  518.5 49.1 %collective-permute-start.3 = (f32[4096,64]{0,1:T(8,128)}, f32[4096,64]{0,1:T(8,128)S(1)}, u32[]{:S(2)}, u32[]{:S(2)}) collective-permute-start(f32[4096,64]{0,1:T(8,128)} %copy.86), channel_id=1, source_target_pairs={{0,2},{1,3},{2,0},{3,1},{4,6},{5,7},{6,4},{7,5},{8,10},{9,11},{10,... | collective-permute-start | bytes 3145736 | tf_op jit(solution)/shard_map/ppermute | solution.py:59
